TPU v7x, 256 devices: a whole 4x4x8 slice. The times are simulated.
256 devices in a mesh: dp: 8 (over z), space: 32 (over x, y, core).
Axes of the slice: x: 4, y: 4, z: 8, core: 2. Of those that a mesh axis runs over, the one named last changes fastest.
Arguments:
- volume: bfloat16 [8, 32, 8, 16, 16, 256], P('dp', 'space'), may hold values from -6 to 6
- fine_filter: bfloat16 [3, 3, 3, 256, 256], P(None, None, None, 'dp'), may hold values from -0.078125 to 0.078125
- coarse_filter: bfloat16 [3, 3, 3, 256, 256], P(None, None, None, 'dp'), may hold values from -0.078125 to 0.078125
- fine_bias: float32 [256], replicated, may hold values from -3 to 3
- coarse_bias: float32 [256], replicated, may hold values from -3 to 3
Outputs:
- context: bfloat16 [8, 32, 8, 16, 16, 256], P('dp', 'space')
All inputs are finite; a program needn't handle non-finite values.
Results may differ from a plain program's by a relative error of at most 0.0047.
Values may be sent and summed in bfloat16 or wider, within the bound.
No kernel may reach another device: no remote copies, remote signals or barrier semaphores. Data moves between devices by JAX's collectives and lax.ppermute only.
A program may use at most 128 MiB of HBM per device.

v0:
```python
import jax
import jax.numpy as jnp
from jax import lax
from jax.sharding import PartitionSpec as P

X = 64
BX = 8


def filters(shard):
    return lax.all_gather(shard, "dp", axis=3, tiled=True)


def dense_taps(grid, weights, bias):
    items, length_x, length_y, length_z, channels = grid.shape
    padded = jnp.pad(grid, ((0, 0), (1, 1), (1, 1), (1, 1), (0, 0)))
    total = jnp.zeros(grid.shape, jnp.float32)
    for step_x in range(3):
        for step_y in range(3):
            window = padded[:, step_x : step_x + length_x, step_y : step_y + length_y]
            stacked = jnp.concatenate(
                [window[:, :, :, depth : depth + length_z] for depth in range(3)], axis=-1
            )
            total = total + jnp.dot(
                stacked,
                weights[step_x, step_y].reshape(3 * channels, channels),
                preferred_element_type=jnp.float32,
            )
    return (grid.astype(jnp.float32) + jax.nn.gelu(total + bias)).astype(jnp.bfloat16)


def fine_cosets(brick):
    size_x, size_y, size_z, channels = brick.shape
    split = brick.reshape(size_x // 4, 4, size_y // 4, 4, size_z // 4, 4, channels)
    return split.transpose(1, 3, 5, 0, 2, 4, 6).reshape(
        64, size_x // 4, size_y // 4, size_z // 4, channels
    )


def fine_bricks(cosets):
    count, along_u, along_v, along_w, channels = cosets.shape
    split = cosets.reshape(4, 4, 4, along_u, along_v, along_w, channels).transpose(
        3, 0, 4, 1, 5, 2, 6
    )
    return split.reshape(along_u * 4, along_v * 4, along_w * 4, channels)


def assemble(parts):
    items, devices, along_u, along_v, along_w, channels = parts.shape
    across_x = X // BX
    across_y = devices // across_x
    grid = parts.reshape(items, across_x, across_y, along_u, along_v, along_w, channels).transpose(
        0, 1, 3, 2, 4, 5, 6
    )
    return grid.reshape(items, across_x * along_u, across_y * along_v, along_w, channels)


def disassemble(grid, along_u, along_v):
    items, size_x, size_y, along_w, channels = grid.shape
    across_x = size_x // along_u
    across_y = size_y // along_v
    parts = grid.reshape(items, across_x, along_u, across_y, along_v, along_w, channels).transpose(
        0, 1, 3, 2, 4, 5, 6
    )
    return parts.reshape(1, items, across_x * across_y, along_u, along_v, along_w, channels)


def split_halves(grid):
    items, size_x, size_y, size_z, channels = grid.shape
    parts = grid.reshape(items, size_x // 2, 2, size_y // 2, 2, size_z // 2, 2, channels).transpose(
        0, 2, 4, 6, 1, 3, 5, 7
    )
    return parts.reshape(items * 8, size_x // 2, size_y // 2, size_z // 2, channels)


def join_halves(parts, items):
    count, half_x, half_y, half_z, channels = parts.shape
    grid = parts.reshape(items, 2, 2, 2, half_x, half_y, half_z, channels).transpose(
        0, 4, 1, 5, 2, 6, 3, 7
    )
    return grid.reshape(items, half_x * 2, half_y * 2, half_z * 2, channels)


def on_device(volume, fine_filter, coarse_filter, fine_bias, coarse_bias):
    brick = volume[0, 0]
    devices = lax.axis_size("space")
    fine_weights = filters(fine_filter)
    coarse_weights = filters(coarse_filter)
    cosets = fine_cosets(brick)
    outgoing = cosets.reshape((devices, 64 // devices, 1) + cosets.shape[1:])
    received = lax.all_to_all(outgoing, "space", split_axis=0, concat_axis=2, tiled=True)
    items = received.shape[1]
    along_u = received.shape[3]
    along_v = received.shape[4]
    grid = dense_taps(assemble(received[0]), fine_weights, fine_bias)
    finer = dense_taps(split_halves(grid), coarse_weights, coarse_bias)
    grid = join_halves(finer, items)
    returned = lax.all_to_all(
        disassemble(grid, along_u, along_v), "space", split_axis=2, concat_axis=0, tiled=True
    )
    brick = fine_bricks(returned.reshape(cosets.shape))
    return brick.reshape(volume.shape)


def solution(mesh):
    return jax.shard_map(
        on_device,
        mesh=mesh,
        in_specs=(
            P("dp", "space", None, None, None, None),
            P(None, None, None, "dp", None),
            P(None, None, None, "dp", None),
            P(),
            P(),
        ),
        out_specs=P("dp", "space", None, None, None, None),
        check_vma=False,
    )
```

profile of v0, /device:TPU:1, one launch (start us, length us, event | category | flops | bytes accessed | tf_op | source)
XLA Modules:
  0.0 164.3 jit_solution(2453152711800644022)
XLA Ops:
  6.5 0.7 all-gather.3.cloned.1.call-update
  7.3 1.3 reshape_squeeze.60
  8.6 1.6 copy.22
  10.2 8.6 %all-to-all-start = ((bf16[32,2,1,2,4,4,256]{6,5,4,3,1,2,0:T(4,128)(2,1)}), bf16[32,2,1,2,4,4,256]{6,5,4,3,1,2,0:T(4,128)(2,1)S(1)}, u32[]{:S(2)}, u32[]{:S(2)}) async-start(bf16[32,2,1,2,4,4,256]{6,5,4,3,1,2,0:T(4,128)(2,1)} %bitcast.2), calls=%async_computation | async-start | bytes 2097152 | tf_op jit(solution)/shard_map/all_to_all | solution.py:91
  18.8 0.7 all-gather.5.cloned.1.call-update
  19.5 16.2 %all-to-all-done = bf16[32,2,1,2,4,4,256]{6,5,4,3,1,2,0:T(4,128)(2,1)S(1)} async-done(((bf16[32,2,1,2,4,4,256]{6,5,4,3,1,2,0:T(4,128)(2,1)}), bf16[32,2,1,2,4,4,256]{6,5,4,3,1,2,0:T(4,128)(2,1)S(1)}, u32[]{:S(2)}, u32[]{:S(2)}) %all-to-all-start) | async-done | bytes 1048608 | tf_op jit(solution)/shard_map/all_to_all | solution.py:91
  35.7 0.5 copy.25
  36.5 3.2 %pad_slice_fusion.27 = (bf16[2,16,16,4,256]{4,2,3,1,0:T(8,128)(2,1)}, bf16[2,16,16,4,256]{4,2,3,1,0:T(8,128)(2,1)}, bf16[2,16,16,4,256]{4,2,3,1,0:T(8,128)(2,1)}...) fusion(bf16[2,16,16,4,256]{4,2,3,1,0:T(8,128)(2,1)S(1)} %reshape.19), kind=kLoop, calls=%fused_computation.27 | loop fusion | bytes 8388608 | tf_op jit(solution)/shard_map/slice | solution.py:22
  39.7 6.7 %pad_slice_fusion.28 = (bf16[2,16,16,4,256]{4,2,3,1,0:T(8,128)(2,1)S(1)}, bf16[2,16,16,4,256]{4,2,3,1,0:T(8,128)(2,1)}, bf16[2,16,16,4,256]{4,2,3,1,0:T(8,128)(2...) fusion(bf16[2,16,16,4,256]{4,2,3,1,0:T(8,128)(2,1)S(1)} %reshape.19), kind=kLoop, calls=%fused_computation.28 | loop fusion | bytes 20971520 | tf_op jit(solution)/shard_map/slice | solution.py:22
  46.5 14.9 %all-gather.3.cloned.1.call-done = bf16[3,3,3,256,256]{4,3,2,1,0:T(8,128)(2,1)} async-done(((bf16[3,3,3,32,256]{4,3,2,1,0:T(8,128)(2,1)}), bf16[3,3,3,256,256]{4,3,2,1,0:T(8,128)(2,1)}) %all-gather.3.cloned.1.call-update) | async-done | bytes 3538960 | tf_op jit(solution)/shard_map/all_gather | solution.py:11
  61.4 2.3 %fusion.149 = (bf16[1,1,3,256,256]{4,3,2,1,0:T(8,128)(2,1)S(1)}, bf16[1,1,3,256,256]{4,3,2,1,0:T(8,128)(2,1)S(1)}, bf16[1,1,3,256,256]{4,3,2,1,0:T(8,128)(2,1)S(...) fusion(bf16[3,3,3,256,256]{4,3,2,1,0:T(8,128)(2,1)} %all-gather, ...), kind=kLoop, calls=%fused_computation.199 | loop fusion | bytes 7077888 | tf_op jit(solution)/shard_map/slice | solution.py:26
  64.0 1.2 fusion.24
  65.2 0.3 copy-done.29
  65.5 0.3 copy-done.30
  65.9 1.2 fusion.6
  67.1 0.3 copy-done.26
  67.4 0.3 copy-done.27
  67.7 1.2 fusion.12
  69.6 1.2 fusion.18
  71.4 1.2 fusion.30
  72.6 0.3 copy-done.7
  73.3 1.2 fusion
  74.8 1.2 fusion.36
  76.0 0.3 copy-done.39
  76.7 1.2 fusion.42
  78.2 2.1 %fusion.116 = bf16[2,16,16,4,256]{4,2,3,1,0:T(8,128)(2,1)S(1)} fusion(f32[2,16,16,4,256]{4,2,3,1,0:T(8,128)S(1)} %fusion.42, f32[2,16,16,4,256]{4,2,3,1,0:T(8,128)S(1)} %fusion.36, f32[2,16,16,4,256]{4,2,3,1,0:T(8,128)S(1)} %fusion.30, f32[2,16,16,4,256]{4,2,3,1,0:T(8,128)S(1)} %fusion.24, f32[2,16,16,4,256]{4,2,3,1,0:T(8,128)S(1)} %fusion.18, ...), kind=kOutput, calls=%fused_computation.170 | convolution fusion | flops 825229312 | bytes 22414336 | tf_op jit(solution)/shard_map/dot_general | solution.py:24
  80.4 0.4 reshape.20
  81.0 2.8 %pad_slice_fusion.1 = (bf16[16,8,8,2,256]{4,2,3,1,0:T(8,128)(2,1)S(1)}, bf16[16,8,8,2,256]{4,2,3,1,0:T(8,128)(2,1)}, bf16[16,8,8,2,256]{4,2,3,1,0:T(8,128)(2,1)}...) fusion(bf16[16,8,8,2,256]{4,2,3,1,0:T(8,128)(2,1)S(1)} %bitcast.145), kind=kLoop, calls=%fused_computation.1 | loop fusion | bytes 8388608 | tf_op jit(solution)/shard_map/slice | solution.py:22
  83.8 6.5 %pad_slice_fusion.2 = (bf16[16,8,8,2,256]{4,2,3,1,0:T(8,128)(2,1)S(1)}, bf16[16,8,8,2,256]{4,2,3,1,0:T(8,128)(2,1)}, bf16[16,8,8,2,256]{4,2,3,1,0:T(8,128)(2,1)}...) fusion(bf16[16,8,8,2,256]{4,2,3,1,0:T(8,128)(2,1)S(1)} %bitcast.146), kind=kLoop, calls=%fused_computation.2 | loop fusion | bytes 20971520 | tf_op jit(solution)/shard_map/slice | solution.py:22
  90.3 20.1 %all-gather.5.cloned.1.call-done = bf16[3,3,3,256,256]{4,3,2,1,0:T(8,128)(2,1)} async-done(((bf16[3,3,3,32,256]{4,3,2,1,0:T(8,128)(2,1)}), bf16[3,3,3,256,256]{4,3,2,1,0:T(8,128)(2,1)}) %all-gather.5.cloned.1.call-update) | async-done | bytes 3538960 | tf_op jit(solution)/shard_map/all_gather | solution.py:11
  110.4 2.4 %fusion.148 = (bf16[1,1,3,256,256]{4,3,2,1,0:T(8,128)(2,1)S(1)}, bf16[1,1,3,256,256]{4,3,2,1,0:T(8,128)(2,1)S(1)}, bf16[1,1,3,256,256]{4,3,2,1,0:T(8,128)(2,1)S(...) fusion(bf16[3,3,3,256,256]{4,3,2,1,0:T(8,128)(2,1)} %all-gather, ...), kind=kLoop, calls=%fused_computation.198 | loop fusion | bytes 7077888 | tf_op jit(solution)/shard_map/slice | solution.py:26
  113.0 1.2 fusion.78
  114.3 0.3 copy-done.32
  114.9 1.2 fusion.60
  116.8 1.2 fusion.54
  118.6 1.2 fusion.66
  120.5 1.2 fusion.72
  122.0 0.3 copy-done.10
  122.3 1.2 fusion.84
  123.9 0.3 copy-done.45
  124.2 1.2 fusion.90
  126.0 1.2 fusion.96
  127.3 2.3 %fusion.125 = bf16[16,8,8,2,256]{4,2,3,1,0:T(8,128)(2,1)S(1)} fusion(f32[16,8,8,2,256]{4,2,3,1,0:T(8,128)S(1)} %fusion.96, f32[16,8,8,2,256]{4,2,3,1,0:T(8,128)S(1)} %fusion.90, f32[16,8,8,2,256]{4,2,3,1,0:T(8,128)S(1)} %fusion.84, f32[16,8,8,2,256]{4,2,3,1,0:T(8,128)S(1)} %fusion.78, f32[16,8,8,2,256]{4,2,3,1,0:T(8,128)S(1)} %fusion.72, ...), kind=kOutput, calls=%fused_computation.179 | convolution fusion | flops 825229312 | bytes 22414336 | tf_op jit(solution)/shard_map/dot_general | solution.py:24
  129.6 0.4 copy.27
  130.0 0.6 copy.50
  130.6 24.4 %all_to_all.30 = bf16[1,2,32,2,4,4,256]{6,5,4,3,1,0,2:T(4,128)(2,1)S(1)} all-to-all(bf16[1,2,32,2,4,4,256]{6,5,4,3,1,0,2:T(4,128)(2,1)S(1)} %bitcast.153), channel_id=1, replica_groups=mesh['dp'=8,'space'=32] {'space'}, dimensions={2} | all-to-all | bytes 2097152 | tf_op jit(solution)/shard_map/all_to_all | solution.py:98
  155.0 1.4 copy.30
  156.4 1.1 reshape_reshape.15
  (95 shorter events, 7.4 us)
Async XLA Ops:
  6.5 54.9 %all-gather.3.cloned.1.call-start = ((), (), s32[]{:S(2)}) async-start(), calls=%async_computation.2 | async-start | bytes 3981312 | tf_op jit(solution)/shard_map/all_gather | solution.py:11
  10.2 25.5 %all-to-all-start = ((bf16[32,2,1,2,4,4,256]{6,5,4,3,1,2,0:T(4,128)(2,1)}), bf16[32,2,1,2,4,4,256]{6,5,4,3,1,2,0:T(4,128)(2,1)S(1)}, u32[]{:S(2)}, u32[]{:S(2)}) async-start(bf16[32,2,1,2,4,4,256]{6,5,4,3,1,2,0:T(4,128)(2,1)} %bitcast.2), calls=%async_computation | async-start | bytes 2097152 | tf_op jit(solution)/shard_map/all_to_all | solution.py:91
  18.8 91.7 %all-gather.5.cloned.1.call-start = ((), (), s32[]{:S(2)}) async-start(), calls=%async_computation.3 | async-start | bytes 3981312 | tf_op jit(solution)/shard_map/all_gather | solution.py:11
  61.4 2.3 %copy-start.34 = (bf16[2,16,16,4,256]{4,2,3,1,0:T(8,128)(2,1)S(1)}, bf16[2,16,16,4,256]{4,2,3,1,0:T(8,128)(2,1)}, u32[]{:S(2)}) copy-start(bf16[2,16,16,4,256]{4,2,3,1,0:T(8,128)(2,1)} %get-tuple-element.61) | copy-start | bytes 3145732
  61.4 2.6 %copy-start.35 = (bf16[2,16,16,4,256]{4,2,3,1,0:T(8,128)(2,1)S(1)}, bf16[2,16,16,4,256]{4,2,3,1,0:T(8,128)(2,1)}, u32[]{:S(2)}) copy-start(bf16[2,16,16,4,256]{4,2,3,1,0:T(8,128)(2,1)} %get-tuple-element.62) | copy-start | bytes 3145732
  64.0 1.2 copy-start.28
  64.0 1.5 copy-start.29
  64.0 1.9 %copy-start.30 = (bf16[2,16,16,4,256]{4,2,3,1,0:T(8,128)(2,1)S(1)}, bf16[2,16,16,4,256]{4,2,3,1,0:T(8,128)(2,1)}, u32[]{:S(2)}) copy-start(bf16[2,16,16,4,256]{4,2,3,1,0:T(8,128)(2,1)} %get-tuple-element.54) | copy-start | bytes 3145732
  65.9 1.2 copy-start.25
  65.9 1.5 copy-start.26
  65.9 1.9 %copy-start.27 = (bf16[2,16,16,4,256]{4,2,3,1,0:T(8,128)(2,1)S(1)}, bf16[2,16,16,4,256]{4,2,3,1,0:T(8,128)(2,1)}, u32[]{:S(2)}) copy-start(bf16[2,16,16,4,256]{4,2,3,1,0:T(8,128)(2,1)} %get-tuple-element.57) | copy-start | bytes 3145732
  67.7 1.2 copy-start.20
  67.7 1.5 copy-start.21
  67.7 1.9 %copy-start.22 = (bf16[2,16,16,4,256]{4,2,3,1,0:T(8,128)(2,1)S(1)}, bf16[2,16,16,4,256]{4,2,3,1,0:T(8,128)(2,1)}, u32[]{:S(2)}) copy-start(bf16[2,16,16,4,256]{4,2,3,1,0:T(8,128)(2,1)} %get-tuple-element.60) | copy-start | bytes 3145732
  69.6 1.2 copy-start.14
  69.6 1.5 copy-start.15
  69.6 1.9 %copy-start.16 = (bf16[2,16,16,4,256]{4,2,3,1,0:T(8,128)(2,1)S(1)}, bf16[2,16,16,4,256]{4,2,3,1,0:T(8,128)(2,1)}, u32[]{:S(2)}) copy-start(bf16[2,16,16,4,256]{4,2,3,1,0:T(8,128)(2,1)} %get-tuple-element.65) | copy-start | bytes 3145732
  71.4 1.2 copy-start.6
  71.4 1.5 copy-start.7
  71.4 1.9 %copy-start.46 = (bf16[2,16,16,4,256]{4,2,3,1,0:T(8,128)(2,1)S(1)}, bf16[2,16,16,4,256]{4,2,3,1,0:T(8,128)(2,1)}, u32[]{:S(2)}) copy-start(bf16[2,16,16,4,256]{4,2,3,1,0:T(8,128)(2,1)} %get-tuple-element.74) | copy-start | bytes 3145732
  73.3 1.2 copy-start.3
  73.3 1.5 copy-start.44
  74.8 1.2 copy-start.38
  74.8 1.5 copy-start.39
  74.8 1.9 %copy-start.40 = (bf16[2,16,16,4,256]{4,2,3,1,0:T(8,128)(2,1)S(1)}, bf16[2,16,16,4,256]{4,2,3,1,0:T(8,128)(2,1)}, u32[]{:S(2)}) copy-start(bf16[2,16,16,4,256]{4,2,3,1,0:T(8,128)(2,1)} %get-tuple-element.72) | copy-start | bytes 3145732
  76.7 1.2 copy-start
  76.7 1.5 copy-start.1
  76.7 1.5 copy-start.48
  110.4 2.4 %copy-start.36 = (bf16[16,8,8,2,256]{4,2,3,1,0:T(8,128)(2,1)S(1)}, bf16[16,8,8,2,256]{4,2,3,1,0:T(8,128)(2,1)}, u32[]{:S(2)}) copy-start(bf16[16,8,8,2,256]{4,2,3,1,0:T(8,128)(2,1)} %get-tuple-element.35) | copy-start | bytes 3145732
  110.4 2.6 %copy-start.37 = (bf16[16,8,8,2,256]{4,2,3,1,0:T(8,128)(2,1)S(1)}, bf16[16,8,8,2,256]{4,2,3,1,0:T(8,128)(2,1)}, u32[]{:S(2)}) copy-start(bf16[16,8,8,2,256]{4,2,3,1,0:T(8,128)(2,1)} %get-tuple-element.36) | copy-start | bytes 3145732
  113.0 1.2 copy-start.31
  113.0 1.5 copy-start.32
  113.0 1.9 %copy-start.33 = (bf16[16,8,8,2,256]{4,2,3,1,0:T(8,128)(2,1)S(1)}, bf16[16,8,8,2,256]{4,2,3,1,0:T(8,128)(2,1)}, u32[]{:S(2)}) copy-start(bf16[16,8,8,2,256]{4,2,3,1,0:T(8,128)(2,1)} %get-tuple-element.28) | copy-start | bytes 3145732
  114.9 1.2 copy-start.23
  114.9 1.5 copy-start.24
  114.9 1.9 %copy-start.47 = (bf16[16,8,8,2,256]{4,2,3,1,0:T(8,128)(2,1)S(1)}, bf16[16,8,8,2,256]{4,2,3,1,0:T(8,128)(2,1)}, u32[]{:S(2)}) copy-start(bf16[16,8,8,2,256]{4,2,3,1,0:T(8,128)(2,1)} %get-tuple-element.48) | copy-start | bytes 3145732
  116.8 1.5 copy-start.18
  116.8 1.9 %copy-start.19 = (bf16[16,8,8,2,256]{4,2,3,1,0:T(8,128)(2,1)S(1)}, bf16[16,8,8,2,256]{4,2,3,1,0:T(8,128)(2,1)}, u32[]{:S(2)}) copy-start(bf16[16,8,8,2,256]{4,2,3,1,0:T(8,128)(2,1)} %get-tuple-element.31) | copy-start | bytes 3145732
  118.6 1.5 copy-start.12
  118.6 1.9 %copy-start.13 = (bf16[16,8,8,2,256]{4,2,3,1,0:T(8,128)(2,1)S(1)}, bf16[16,8,8,2,256]{4,2,3,1,0:T(8,128)(2,1)}, u32[]{:S(2)}) copy-start(bf16[16,8,8,2,256]{4,2,3,1,0:T(8,128)(2,1)} %get-tuple-element.34) | copy-start | bytes 3145732
  120.5 1.2 copy-start.8
  120.5 1.5 copy-start.9
  120.5 1.9 %copy-start.10 = (bf16[16,8,8,2,256]{4,2,3,1,0:T(8,128)(2,1)S(1)}, bf16[16,8,8,2,256]{4,2,3,1,0:T(8,128)(2,1)}, u32[]{:S(2)}) copy-start(bf16[16,8,8,2,256]{4,2,3,1,0:T(8,128)(2,1)} %get-tuple-element.39) | copy-start | bytes 3145732
  122.3 1.5 copy-start.5
  122.3 1.9 %copy-start.45 = (bf16[16,8,8,2,256]{4,2,3,1,0:T(8,128)(2,1)S(1)}, bf16[16,8,8,2,256]{4,2,3,1,0:T(8,128)(2,1)}, u32[]{:S(2)}) copy-start(bf16[16,8,8,2,256]{4,2,3,1,0:T(8,128)(2,1)} %get-tuple-element.43) | copy-start | bytes 3145732
  124.2 1.5 copy-start.42
  124.2 1.9 %copy-start.43 = (bf16[16,8,8,2,256]{4,2,3,1,0:T(8,128)(2,1)S(1)}, bf16[16,8,8,2,256]{4,2,3,1,0:T(8,128)(2,1)}, u32[]{:S(2)}) copy-start(bf16[16,8,8,2,256]{4,2,3,1,0:T(8,128)(2,1)} %get-tuple-element.46) | copy-start | bytes 3145732
  126.0 1.2 copy-start.49
  (5 other events, 6.1 us)
Sparse Core Ops, SparseCore 0:
  9.1 52.2 all-gather.2
  63.2 47.2 all-gather.4
where the time goes:
time: 165 us; the launch traced here: 164 us
  waiting for transfers between devices  52.6 us (32%)
  local copies, waits for them, and re-layouts  41.6 us (25%)
  blocking collectives  24.4 us (15%)
  matrix products  23.4 us (14%)
  between operations  13.7 us (8%)
  starting transfers between devices  8.62 us (5%)
    all_gather x2, waiting for transfers between devices, filters(): return lax.all_gather(shard, 'dp', axis=3, tiled=True)  35 us
    all_to_all x1, blocking collectives, on_device(): lax.all_to_all(disassemble(grid, along_u, along_v), 'space', split_axis=2...  24.4 us
    dot_general x18, matrix products, dense_taps(): jnp.dot(stacked, weights[step_x, step_y].reshape(3 * channels, channels),...  23.4 us
    slice x4, local copies, waits for them, and re-layouts, dense_taps(): window[:, :, :, depth:depth + length_z]  19.3 us
    all_to_all x1, waiting for transfers between devices, on_device(): lax.all_to_all(outgoing, 'space', split_axis=0, concat_axis=2, tiled=True)  16.2 us
    unnamed x100, local copies, waits for them, and re-layouts  9.78 us
    all_to_all x1, starting transfers between devices, on_device(): lax.all_to_all(outgoing, 'space', split_axis=0, concat_axis=2, tiled=True)  8.58 us
    slice x2, local copies, waits for them, and re-layouts, dense_taps(): weights[step_x, step_y].reshape(3 * channels, channels)  4.72 us
  transfers between devices with their start and end apart: 3, of which 3 were waited for; matrix products, arithmetic and copies ran while one was open for 23% of the time, Pallas kernels for 0%

commit v1 on v0

--- a/solution.py
+++ b/solution.py
@@ -8,7 +8,9 @@
 
 
 def filters(shard):
-    return lax.all_gather(shard, "dp", axis=3, tiled=True)
+    return jnp.concatenate(
+        lax.all_to_all(jnp.stack([shard] * lax.axis_size("dp")), "dp", 0, 0), axis=3
+    )
 
 
 def dense_taps(grid, weights, bias):

time: 165 us -> 253 us (1.53)
  waiting for transfers between devices: 52.6 us -> 122 us
  blocking collectives: 24.4 us -> 46 us
  between operations: 13.7 us -> 0.36 us
  local copies, waits for them, and re-layouts: 41.6 us -> 46.1 us
  starting transfers between devices: 8.62 us -> 12.8 us
    all_to_all x1 -> x2, waiting for transfers between devices: 16.2 us -> 122 us  [filters(): lax.all_to_all(jnp.stack([shard] * lax.axis_size('dp')), 'dp', 0, 0)]
    all_gather x2 -> x0, waiting for transfers between devices: 35 us -> none  [filters(): return lax.all_gather(shard, 'dp', axis=3, tiled=True)]
    all_to_all x0 -> x1, blocking collectives: none -> 25.3 us  [on_device(): lax.all_to_all(outgoing, 'space', split_axis=0, concat_axis=2, tiled=True)]
    all_to_all x0 -> x2, local copies, waits for them, and re-layouts: none -> 4.78 us  [filters(): lax.all_to_all(jnp.stack([shard] * lax.axis_size('dp')), 'dp', 0, 0)]
    another operation x0 -> x2, local copies, waits for them, and re-layouts: none -> 4.43 us  [filters(): jnp.stack([shard] * lax.axis_size('dp'))]
    all_to_all x1 -> x2, starting transfers between devices: 8.58 us -> 12.8 us  [filters(): lax.all_to_all(jnp.stack([shard] * lax.axis_size('dp')), 'dp', 0, 0)]
    slice x2, local copies, waits for them, and re-layouts: 4.72 us -> 0.53 us  [dense_taps(): weights[step_x, step_y].reshape(3 * channels, channels)]
    all_to_all x1, blocking collectives: 24.4 us -> 20.7 us  [on_device(): lax.all_to_all(disassemble(grid, along_u, along_v), 'space', split_axis=2...]
  transfers between devices with their start and end apart: 3 -> 2, of which waited for: 3 -> 2; matrix products, arithmetic and copies ran while one was open for 23% -> 14% of each run, Pallas kernels for 0% -> 0%
where the time goes in v1:
time: 253 us; the launch traced here: 251 us
  waiting for transfers between devices  122 us (48%)
  local copies, waits for them, and re-layouts  46.1 us (18%)
  blocking collectives  46 us (18%)
  matrix products  23.5 us (9%)
  starting transfers between devices  12.8 us (5%)
    all_to_all x2, waiting for transfers between devices, filters(): lax.all_to_all(jnp.stack([shard] * lax.axis_size('dp')), 'dp', 0, 0)  122 us
    all_to_all x1, blocking collectives, on_device(): lax.all_to_all(outgoing, 'space', split_axis=0, concat_axis=2, tiled=True)  25.3 us
    dot_general x18, matrix products, dense_taps(): jnp.dot(stacked, weights[step_x, step_y].reshape(3 * channels, channels),...  23.5 us
    all_to_all x1, blocking collectives, on_device(): lax.all_to_all(disassemble(grid, along_u, along_v), 'space', split_axis=2...  20.7 us
    slice x4, local copies, waits for them, and re-layouts, dense_taps(): window[:, :, :, depth:depth + length_z]  18.7 us
    all_to_all x2, starting transfers between devices, filters(): lax.all_to_all(jnp.stack([shard] * lax.axis_size('dp')), 'dp', 0, 0)  12.8 us
    unnamed x96, local copies, waits for them, and re-layouts  10.8 us
  transfers between devices with their start and end apart: 2, of which 2 were waited for; matrix products, arithmetic and copies ran while one was open for 14% of the time, Pallas kernels for 0%

profile of v1, /device:TPU:1, one launch (start us, length us, event | category | flops | bytes accessed | tf_op | source)
XLA Modules:
  0.0 251.0 jit_solution(16018811452094055711)
XLA Ops:
  0.0 1.4 reshape_squeeze.60
  1.4 0.6 copy.31
  2.0 25.3 %all_to_all.40 = bf16[32,2,1,2,4,4,256]{6,5,4,3,1,2,0:T(4,128)(2,1)S(1)} all-to-all(bf16[32,2,1,2,4,4,256]{6,5,4,3,1,2,0:T(4,128)(2,1)S(1)} %bitcast.159), channel_id=1, replica_groups=mesh['dp'=8,'space'=32] {'space'}, dimensions={0} | all-to-all | bytes 2097152 | tf_op jit(solution)/shard_map/all_to_all | solution.py:93
  27.3 2.2 stack.4
  29.5 8.2 %all-to-all-start.1 = ((bf16[8,3,3,3,32,256]{5,4,3,2,1,0:T(8,128)(2,1)}), bf16[8,3,3,3,32,256]{5,4,3,2,1,0:T(8,128)(2,1)}, u32[]{:S(2)}, u32[]{:S(2)}) async-start(bf16[8,3,3,3,32,256]{5,4,3,2,1,0:T(8,128)(2,1)} %stack.4), calls=%async_computation.1 | async-start | bytes 7077888 | tf_op jit(solution)/shard_map/all_to_all | solution.py:12
  37.7 0.5 copy.34
  38.6 82.0 %all-to-all-done.1 = bf16[8,3,3,3,32,256]{5,4,3,2,1,0:T(8,128)(2,1)} async-done(((bf16[8,3,3,3,32,256]{5,4,3,2,1,0:T(8,128)(2,1)}), bf16[8,3,3,3,32,256]{5,4,3,2,1,0:T(8,128)(2,1)}, u32[]{:S(2)}, u32[]{:S(2)}) %all-to-all-start.1) | async-done | bytes 3538976 | tf_op jit(solution)/shard_map/all_to_all | solution.py:12
  120.5 2.2 stack.5
  122.8 4.7 %all-to-all-start.2 = ((bf16[8,3,3,3,32,256]{5,4,3,2,1,0:T(8,128)(2,1)}), bf16[8,3,3,3,32,256]{5,4,3,2,1,0:T(8,128)(2,1)}, u32[]{:S(2)}, u32[]{:S(2)}) async-start(bf16[8,3,3,3,32,256]{5,4,3,2,1,0:T(8,128)(2,1)} %stack.5), calls=%async_computation.2 | async-start | bytes 7077888 | tf_op jit(solution)/shard_map/all_to_all | solution.py:12
  127.4 2.8 %pad_slice_fusion.27 = (bf16[2,16,16,4,256]{4,2,3,1,0:T(8,128)(2,1)S(1)}, bf16[2,16,16,4,256]{4,2,3,1,0:T(8,128)(2,1)}, bf16[2,16,16,4,256]{4,2,3,1,0:T(8,128)(2...) fusion(bf16[2,16,16,4,256]{4,2,3,1,0:T(8,128)(2,1)S(1)} %reshape.35), kind=kLoop, calls=%fused_computation.27 | loop fusion | bytes 8388608 | tf_op jit(solution)/shard_map/slice | solution.py:24
  130.2 6.5 %pad_slice_fusion.28 = (bf16[2,16,16,4,256]{4,2,3,1,0:T(8,128)(2,1)S(1)}, bf16[2,16,16,4,256]{4,2,3,1,0:T(8,128)(2,1)S(1)}, bf16[2,16,16,4,256]{4,2,3,1,0:T(8,12...) fusion(bf16[2,16,16,4,256]{4,2,3,1,0:T(8,128)(2,1)S(1)} %reshape.35), kind=kLoop, calls=%fused_computation.28 | loop fusion | bytes 20971520 | tf_op jit(solution)/shard_map/slice | solution.py:24
  136.7 2.4 copy.35
  139.4 0.9 copy-done.32
  140.4 0.3 copy-done.33
  140.7 1.2 fusion.24
  141.9 0.3 copy-done.30
  142.2 0.3 copy-done.31
  142.5 1.2 fusion.6
  144.1 0.3 copy-done.28
  144.4 1.2 fusion.12
  146.3 1.2 fusion.18
  148.1 1.2 fusion.30
  149.6 1.2 fusion
  150.9 1.2 fusion.36
  152.7 1.2 fusion.42
  153.9 2.2 fusion.116
  156.1 0.4 reshape.38
  156.7 2.8 %pad_slice_fusion.1 = (bf16[16,8,8,2,256]{4,2,3,1,0:T(8,128)(2,1)S(1)}, bf16[16,8,8,2,256]{4,2,3,1,0:T(8,128)(2,1)}, bf16[16,8,8,2,256]{4,2,3,1,0:T(8,128)(2,1)}...) fusion(bf16[16,8,8,2,256]{4,2,3,1,0:T(8,128)(2,1)S(1)} %bitcast.151), kind=kLoop, calls=%fused_computation.1 | loop fusion | bytes 8388608 | tf_op jit(solution)/shard_map/slice | solution.py:24
  159.5 6.6 %pad_slice_fusion.2 = (bf16[16,8,8,2,256]{4,2,3,1,0:T(8,128)(2,1)S(1)}, bf16[16,8,8,2,256]{4,2,3,1,0:T(8,128)(2,1)}, bf16[16,8,8,2,256]{4,2,3,1,0:T(8,128)(2,1)}...) fusion(bf16[16,8,8,2,256]{4,2,3,1,0:T(8,128)(2,1)S(1)} %bitcast.152), kind=kLoop, calls=%fused_computation.2 | loop fusion | bytes 20971520 | tf_op jit(solution)/shard_map/slice | solution.py:24
  166.1 40.2 %all-to-all-done.2 = bf16[8,3,3,3,32,256]{5,4,3,2,1,0:T(8,128)(2,1)} async-done(((bf16[8,3,3,3,32,256]{5,4,3,2,1,0:T(8,128)(2,1)}), bf16[8,3,3,3,32,256]{5,4,3,2,1,0:T(8,128)(2,1)}, u32[]{:S(2)}, u32[]{:S(2)}) %all-to-all-start.2) | async-done | bytes 3538976 | tf_op jit(solution)/shard_map/all_to_all | solution.py:12
  206.3 2.4 copy.37
  209.0 0.9 copy-done.24
  209.9 0.3 copy-done.25
  210.2 1.2 fusion.78
  212.1 1.2 fusion.60
  213.9 1.2 fusion.54
  215.8 1.2 fusion.66
  217.7 1.2 fusion.72
  219.2 0.3 copy-done.5
  219.5 1.2 fusion.84
  221.4 1.2 fusion.90
  223.2 1.2 fusion.96
  224.4 2.3 fusion.125
  226.8 0.4 copy.38
  227.2 0.6 copy.61
  227.8 20.7 %all_to_all.41 = bf16[1,2,32,2,4,4,256]{6,5,4,3,1,0,2:T(4,128)(2,1)S(1)} all-to-all(bf16[1,2,32,2,4,4,256]{6,5,4,3,1,0,2:T(4,128)(2,1)S(1)} %bitcast.162), channel_id=1, replica_groups=mesh['dp'=8,'space'=32] {'space'}, dimensions={2} | all-to-all | bytes 2097152 | tf_op jit(solution)/shard_map/all_to_all | solution.py:100
  248.5 1.4 copy.41
  249.9 1.1 reshape_reshape.15
  (92 shorter events, 8.1 us)
Async XLA Ops:
  0.0 27.3 %copy-start.44 = (bf16[3,3,3,32,256]{4,3,2,1,0:T(8,128)(2,1)S(1)}, bf16[3,3,3,32,256]{4,3,2,1,0:T(8,128)(2,1)}, u32[]{:S(2)}) copy-start(bf16[3,3,3,32,256]{4,3,2,1,0:T(8,128)(2,1)} %param.6) | copy-start | bytes 1327108
  29.5 91.0 %all-to-all-start.1 = ((bf16[8,3,3,3,32,256]{5,4,3,2,1,0:T(8,128)(2,1)}), bf16[8,3,3,3,32,256]{5,4,3,2,1,0:T(8,128)(2,1)}, u32[]{:S(2)}, u32[]{:S(2)}) async-start(bf16[8,3,3,3,32,256]{5,4,3,2,1,0:T(8,128)(2,1)} %stack.4), calls=%async_computation.1 | async-start | bytes 7077888 | tf_op jit(solution)/shard_map/all_to_all | solution.py:12
  37.7 82.8 %copy-start.45 = (bf16[3,3,3,32,256]{4,3,2,1,0:T(8,128)(2,1)S(1)}, bf16[3,3,3,32,256]{4,3,2,1,0:T(8,128)(2,1)}, u32[]{:S(2)}) copy-start(bf16[3,3,3,32,256]{4,3,2,1,0:T(8,128)(2,1)} %param.7) | copy-start | bytes 1327108
  122.8 83.5 %all-to-all-start.2 = ((bf16[8,3,3,3,32,256]{5,4,3,2,1,0:T(8,128)(2,1)}), bf16[8,3,3,3,32,256]{5,4,3,2,1,0:T(8,128)(2,1)}, u32[]{:S(2)}, u32[]{:S(2)}) async-start(bf16[8,3,3,3,32,256]{5,4,3,2,1,0:T(8,128)(2,1)} %stack.5), calls=%async_computation.2 | async-start | bytes 7077888 | tf_op jit(solution)/shard_map/all_to_all | solution.py:12
  139.1 1.2 copy-start.32
  139.1 1.5 copy-start.33
  140.7 1.2 copy-start.29
  140.7 1.5 copy-start.30
  140.7 1.9 copy-start.31
  142.5 1.2 copy-start.26
  142.5 1.5 copy-start.27
  142.5 1.9 copy-start.28
  144.4 1.2 copy-start.21
  144.4 1.5 copy-start.22
  144.4 1.9 copy-start.23
  146.2 1.2 copy-start.15
  146.3 1.5 copy-start.16
  146.3 1.9 copy-start.17
  148.1 1.2 copy-start.12
  148.1 1.5 copy-start.42
  149.6 1.2 copy-start.41
  150.9 1.2 copy-start.38
  150.9 1.5 copy-start.39
  150.9 1.9 copy-start.40
  208.7 1.2 copy-start.24
  208.7 1.5 copy-start.25
  210.2 1.2 copy-start.18
  210.2 1.5 copy-start.19
  210.2 1.9 copy-start.20
  212.1 1.2 copy-start.13
  212.1 1.5 copy-start.14
  212.1 1.9 copy-start.43
  213.9 1.5 copy-start.10
  213.9 1.9 copy-start.11
  215.8 1.2 copy-start.6
  215.8 1.5 copy-start.7
  215.8 1.9 copy-start.8
  217.6 1.2 copy-start.3
  217.6 1.5 copy-start.4
  217.7 1.9 copy-start.5
  219.5 1.2 copy-start.1
  219.5 1.5 copy-start.2
  219.5 1.9 copy-start.37
  221.4 1.2 copy-start.34
  221.4 1.5 copy-start.35
  221.4 1.9 copy-start.36
  223.2 1.2 copy-start
  223.2 1.2 copy-start.47
  (2 other events, 2.4 us)
